TPU v7x, 128 devices: a whole 4x4x4 slice. The times are simulated.
128 devices in a mesh: aa: 4 (over z_lo, core), ba: 32 (over y, z_hi, x).
Axes of the slice: x: 4, y: 4, z: 4 (z_hi: 2, z_lo: 2; z = z_hi * 2 + z_lo), core: 2. Of those that a mesh axis runs over, the one named last changes fastest.
Arguments:
- hidden: bfloat16 [512, 3072], P('aa'), may hold values from -24 to 24
- head_weight: bfloat16 [3072, 32, 4, 512], P(None, 'ba'), as said below
- teacher: bfloat16 [512, 4, 32, 512], P('ba', 'aa'), may hold values from -60 to 250
Outputs:
- divergence: float32 [], replicated
- grad_hidden: bfloat16 [512, 3072], P('aa')
- grad_head: bfloat16 [3072, 32, 4, 512], P('aa', 'ba')
Inputs may be any that keep to these rules, and one draw needn't show every extreme that they name: `head_weight`: entries of order one over the square root of 3072.
All inputs are finite; a program needn't handle non-finite values.
Results may differ from a plain program's by a relative error of at most 0.0049.
Values may be sent and summed in bfloat16 or wider, within the bound.
A program may use at most 128 MiB of HBM per device.

v0:
```python
import jax
import jax.numpy as jnp
from jax import lax
from jax.sharding import PartitionSpec as P

grad_scale = 256.0


def on_device(hidden, head_weight, teacher):
    token_rows = hidden.shape[0]
    model_width = hidden.shape[1]
    vocab_local = head_weight.shape[2] * head_weight.shape[3]
    weight_flat = head_weight.reshape(model_width, vocab_local)
    arrived = lax.all_to_all(
        lax.all_to_all(teacher, "ba", split_axis=2, concat_axis=0, tiled=True),
        "aa",
        split_axis=0,
        concat_axis=1,
        tiled=True,
    )
    target = arrived.reshape(token_rows, vocab_local).astype(jnp.float32)
    student = jnp.dot(hidden, weight_flat, preferred_element_type=jnp.float32)
    student_peak = jnp.max(student, axis=1)
    target_peak = jnp.max(target, axis=1)
    student_peak, target_peak = lax.pmax((student_peak, target_peak), "ba")
    student_total, target_total = lax.psum(
        (
            jnp.sum(jnp.exp(student - student_peak[:, None]), axis=1),
            jnp.sum(jnp.exp(target - target_peak[:, None]), axis=1),
        ),
        "ba",
    )
    log_student = student - student_peak[:, None] - jnp.log(student_total)[:, None]
    log_target = target - target_peak[:, None] - jnp.log(target_total)[:, None]
    student_prob = jnp.exp(log_student)
    target_prob = jnp.exp(log_target)
    summed = lax.psum(jnp.sum(target_prob * (log_target - log_student)), ("aa", "ba"))
    divergence = summed / (token_rows * lax.axis_size("aa"))
    gradient = (grad_scale * (student_prob - target_prob)).astype(jnp.bfloat16)
    partial_hidden = lax.dot_general(
        gradient, weight_flat, (((1,), (1,)), ((), ())), preferred_element_type=jnp.float32
    )
    grad_hidden = lax.psum(partial_hidden, "ba").astype(jnp.bfloat16)
    share_rows = model_width // lax.axis_size("aa")
    grad_flat = lax.psum_scatter(
        lax.dot_general(
            hidden, gradient, (((0,), (0,)), ((), ())), preferred_element_type=jnp.float32
        ),
        "aa",
        scatter_dimension=0,
        tiled=True,
    )
    grad_head = grad_flat.astype(jnp.bfloat16).reshape(
        share_rows, 1, head_weight.shape[2], head_weight.shape[3]
    )
    return (divergence, grad_hidden, grad_head)


def solution(mesh):
    placed = (P("aa", None), P(None, "ba", None, None), P("ba", "aa", None, None))
    return jax.shard_map(
        on_device,
        mesh=mesh,
        in_specs=placed,
        out_specs=(P(), P("aa", None), P("aa", "ba", None, None)),
        check_vma=False,
    )
```

profile of v0, /device:TPU:0, one launch (start us, length us, event | category | flops | bytes accessed | tf_op | source)
XLA Modules:
  0.0 544.9 jit_solution(8068259267595297354)
XLA Ops:
  7.2 0.0 copy-start
  7.2 2.2 copy.15
  9.4 10.7 %all-to-all-start = ((bf16[16,1,32,512]{3,0,1,2:T(8,128)(2,1)}), bf16[16,1,32,512]{3,0,1,2:T(8,128)(2,1)S(1)}, u32[]{:S(2)}, u32[]{:S(2)}) async-start(bf16[16,1,32,512]{3,0,1,2:T(8,128)(2,1)} %copy.15), calls=%async_computation | async-start | bytes 1048576 | tf_op jit(solution)/shard_map/all_to_all | solution.py:15
  20.1 12.9 %copy.21 = bf16[384,8,4,512]{3,1,2,0:T(8,128)(2,1)} copy(bf16[384,8,4,512]{3,2,1,0:T(4,128)(2,1)} %bitcast.30) | data formatting | bytes 25165824
  33.0 0.2 all-to-all-done
  33.2 0.5 broadcast.10
  33.7 1.0 reduce.7
  34.8 1.2 reshape.34
  35.9 3.5 all-to-all-start.1
  39.4 0.0 reduce-scatter.2.cloned.1.call-start
  39.5 0.0 copy-done
  39.5 6.5 %fusion.2 = (f32[128]{0:T(128)S(1)}, f32[128,2048]{1,0:T(8,128)S(1)}) fusion(bf16[128,3072]{1,0:T(8,128)(2,1)S(1)} %copy-done, bf16[3072,2048]{1,0:T(8,128)(2,1)} %bitcast.28), kind=kOutput, calls=%fused_computation.10 | convolution fusion | flops 1610874752 | bytes 14418432 | tf_op jit(solution)/shard_map/dot_general | solution.py:22
  45.9 2.3 all-to-all-done.1
  48.2 0.5 reshape.35
  48.7 1.1 convert_bitcast_fusion
  49.9 1.6 reduce_max.30
  51.5 1.9 copy.18
  53.4 1.3 copy.20
  54.7 97.3 %all-reduce.1 = (f32[128]{0:T(128)S(1)}, f32[128]{0:T(128)S(1)}) all-reduce(f32[128]{0:T(128)S(1)} %get-tuple-element.23, bf16[128]{0:T(256)(128)(2,1)S(1)} %bitcast_reduce_fusion), channel_id=1, replica_groups=mesh['aa'=4,'ba'=32] {'ba'}, use_global_device_ids=true, to_apply=%region_6.0 | all-reduce | flops 256 | bytes 1792 | tf_op jit(solution)/shard_map/pmax | solution.py:25
  152.0 0.3 fusion.1
  152.3 0.3 exponential_reduce_fusion
  152.6 88.9 %all-reduce = (f32[128]{0:T(128)S(1)}, f32[128]{0:T(128)S(1)}) all-reduce(f32[128]{0:T(128)S(1)} %exponential_reduce_fusion, f32[128]{0:T(128)S(1)} %fusion.1), channel_id=1, replica_groups=mesh['aa'=4,'ba'=32] {'ba'}, use_global_device_ids=true, to_apply=%region_8.0 | all-reduce | flops 256 | bytes 2048 | tf_op jit(solution)/shard_map/psum | solution.py:26
  241.5 2.6 multiply_convert_fusion
  244.1 10.1 %convolution_bitcast_fusion = f32[3072,2048]{0,1:T(8,128)} fusion(bf16[128,2048]{1,0:T(8,128)(2,1)S(1)} %get-tuple-element.21, bf16[128,3072]{1,0:T(8,128)(2,1)S(1)} %copy-done), kind=kOutput, calls=%fused_computation | convolution fusion | flops 1610612736 | bytes 26476544 | tf_op jit(solution)/shard_map/dot_general | solution.py:46
  254.2 0.0 reduce-scatter.2.cloned.1.call-update
  254.2 62.3 %psum.30 = f32[]{:T(128)} all-reduce(f32[]{:T(128)} %get-tuple-element.22), channel_id=1, replica_groups=mesh['aa'=4,'ba'=32] {'aa','ba'}, use_global_device_ids=true, to_apply=%region_10.0 | all-reduce | flops 1 | bytes 8 | tf_op jit(solution)/shard_map/psum | solution.py:37
  316.6 0.0 copy-start.1
  316.6 9.0 %fusion.3 = f32[128,3072]{1,0:T(8,128)S(1)} fusion(bf16[128,2048]{1,0:T(8,128)(2,1)S(1)} %get-tuple-element.21, bf16[3072,2048]{1,0:T(8,128)(2,1)} %bitcast.29), kind=kOutput, calls=%fused_computation.11 | convolution fusion | flops 1610612736 | bytes 14680064 | tf_op jit(solution)/shard_map/dot_general | solution.py:40
  326.2 199.7 %all-reduce.3 = bf16[128,3072]{1,0:T(8,128)(2,1)} all-reduce(f32[128,3072]{1,0:T(8,128)S(1)} %fusion.3), channel_id=1, replica_groups=mesh['aa'=4,'ba'=32] {'ba'}, use_global_device_ids=true, to_apply=%region_11.0 | all-reduce | flops 393216 | bytes 2359296 | tf_op jit(solution)/shard_map/psum | solution.py:43
  526.0 0.0 reduce-scatter.2.cloned.1.call-done
  526.0 4.8 convert_element_type.33
  530.7 6.2 %copy.19 = bf16[768,1,4,512]{3,2,1,0:T(4,128)(2,1)} copy(bf16[768,1,4,512]{0,3,2,1:T(8,128)(2,1)} %bitcast.31) | data formatting | bytes 6291456
  536.9 0.0 copy-done.1
  (3 shorter events, 0.0 us)
Async XLA Ops:
  7.2 32.3 %copy-start = (bf16[128,3072]{1,0:T(8,128)(2,1)S(1)}, bf16[128,3072]{1,0:T(8,128)(2,1)}, u32[]{:S(2)}) copy-start(bf16[128,3072]{1,0:T(8,128)(2,1)} %param.3) | copy-start | bytes 2359300
  9.4 23.9 %all-to-all-start = ((bf16[16,1,32,512]{3,0,1,2:T(8,128)(2,1)}), bf16[16,1,32,512]{3,0,1,2:T(8,128)(2,1)S(1)}, u32[]{:S(2)}, u32[]{:S(2)}) async-start(bf16[16,1,32,512]{3,0,1,2:T(8,128)(2,1)} %copy.15), calls=%async_computation | async-start | bytes 1048576 | tf_op jit(solution)/shard_map/all_to_all | solution.py:15
  35.9 12.3 %all-to-all-start.1 = ((bf16[4,2,32768]{2,1,0:T(2,128)(2,1)}), bf16[4,2,32768]{2,1,0:T(2,128)(2,1)S(1)}, u32[]{:S(2)}, u32[]{:S(2)}) async-start(bf16[4,2,32768]{2,1,0:T(2,128)(2,1)} %reshape.34), calls=%async_computation.1 | async-start | bytes 1048576 | tf_op jit(solution)/shard_map/all_to_all | solution.py:14
  39.4 486.5 %reduce-scatter.2.cloned.1.call-start = ((), (), s32[]{:S(2)}) async-start(), calls=%async_computation.3 | async-start | bytes 31457280 | tf_op jit(solution)/shard_map/reduce_scatter | solution.py:45
  316.6 220.3 %copy-start.1 = (bf16[128,3072]{1,0:T(8,128)(2,1)S(1)}, bf16[128,3072]{1,0:T(8,128)(2,1)}, u32[]{:S(2)}) copy-start(bf16[128,3072]{1,0:T(8,128)(2,1)} %param.3) | copy-start | bytes 2359300
Sparse Core Ops, SparseCore 0:
  254.3 242.6 reduce-scatter.1
where the time goes:
time: 546 us; the launch traced here: 545 us
  blocking collectives  448 us (82%)
  local copies, waits for them, and re-layouts  26.7 us (5%)
  matrix products  25.6 us (5%)
  between operations  15.9 us (3%)
  starting transfers between devices  14.3 us (3%)
  other arithmetic  11.8 us (2%)
    psum x1, blocking collectives, on_device(): grad_hidden = lax.psum(partial_hidden, 'ba').astype(jnp.bfloat16)  200 us
    pmax x1, blocking collectives, on_device(): student_peak, target_peak = lax.pmax((student_peak, target_peak), 'ba')  97.3 us
    psum x1, blocking collectives, on_device(): lax.psum((jnp.sum(jnp.exp(student - student_peak[:, None]), axis=1), jnp....  88.9 us
    psum x1, blocking collectives, on_device(): lax.psum(jnp.sum(target_prob * (log_target - log_student)), ('aa', 'ba'))  62.3 us
    unnamed x10, local copies, waits for them, and re-layouts  24.3 us
  transfers between devices with their start and end apart: 3, of which 2 were waited for; matrix products, arithmetic and copies ran while one was open for 5% of the time, Pallas kernels for 0%

commit v1 on v0

v1 whole, which is shorter than its diff:
```python
import functools

import jax
import jax.numpy as jnp
from jax import lax
from jax.experimental import pallas as pl
from jax.experimental.pallas import tpu as pltpu
from jax.sharding import PartitionSpec as P

MESH = pl.DeviceIdType.MESH
F32 = jnp.float32
BF16 = jnp.bfloat16
grad_scale = 256.0
N_CHUNKS = 12
TB = 16
PAD = 128


def lanes_to_rows(row, n):
    return jnp.transpose(jnp.broadcast_to(row, (n, n)))


def kernel(
    n_ba, x_size,
    hid_hbm, w_hbm, t_hbm,
    div_ref, gh_out, gw_out,
    hid, w_raw, w_std, w_tr, t_raw, t_send, t_in, stu, lse_buf,
    hall, gall, acc, gw, part, rs_buf, z_send, z_recv, fin, kl_p, kl_z, kl_a,
    in_sem, w_sem, t_ssem, t_rsem, h_ssem, h_rsem, s_ssem, s_rsem,
    g_ssem, g_rsem, f_ssem, f_rsem, r_ssem, r_rsem, z_ssem, z_rsem, a_ssem, a_rsem,
    kp_ssem, kp_rsem, kz_ssem, kz_rsem, ka_ssem, ka_rsem, o_sem,
):
    a = lax.axis_index("aa")
    b = lax.axis_index("ba")
    width = hid.shape[1]
    rows = hid.shape[0]
    piece = w_raw.shape[3]
    per_a = n_ba // 4
    plane = n_ba // 2
    share = width // 4
    n_fb = plane // per_a
    fb_width = width // n_fb
    chunk = w_raw.shape[1]
    t_owner = b // per_a
    t_slot = b % per_a
    zh = (b // x_size) % 2
    p = (b // (2 * x_size)) * x_size + b % x_size
    half = a // 2

    def plane_peer(q):
        return ((q // x_size) * 2 + zh) * x_size + q % x_size

    b_across = plane_peer(p) + (1 - 2 * zh) * x_size
    core_mate = a + 1 - 2 * (a % 2)
    chip_mate = (a + 2) % 4

    def remote(src, dst, ssem, rsem, to_a, to_b):
        return pltpu.make_async_remote_copy(
            src_ref=src, dst_ref=dst, send_sem=ssem, recv_sem=rsem,
            device_id=(to_a, to_b), device_id_type=MESH,
        )

    t_load = pltpu.make_async_copy(t_hbm.at[:, 0], t_raw, in_sem.at[0])
    h_load = pltpu.make_async_copy(hid_hbm, hid, in_sem.at[1])
    t_load.start()
    h_load.start()

    def w_load(k):
        return pltpu.make_async_copy(
            w_hbm.at[pl.ds(k * chunk, chunk), 0], w_raw.at[k], w_sem.at[k]
        )

    for k in range(N_CHUNKS):
        w_load(k).start()

    barrier = pltpu.get_barrier_semaphore()

    def greet(to_a, to_b):
        pl.semaphore_signal(barrier, inc=1, device_id=(to_a, to_b), device_id_type=MESH)

    def greet_peers(k, c):
        src_a, src_b = k // per_a, a * per_a + k % per_a

        @pl.when(jnp.logical_or(src_a != a, src_b != b))
        def _():
            greet(src_a, src_b)

        @pl.when(k != b)
        def _():
            greet(a, k)

        return c

    lax.fori_loop(0, n_ba, greet_peers, 0)
    for step in range(1, 4):
        greet((a + step) % 4, b)

    t_load.wait()
    t_send[:, :, 0:piece] = pltpu.einshape("tjr->jtr", t_raw[...])

    def t_max(j, m):
        return jnp.maximum(m, t_send[j, :, 0:piece].astype(F32))

    t_peak = lax.fori_loop(1, n_ba, t_max, t_send[0, :, 0:piece].astype(F32))
    t_peak = jnp.max(t_peak, axis=1, keepdims=True)

    def t_sum(j, s):
        return s + jnp.exp(t_send[j, :, 0:piece].astype(F32) - t_peak)

    t_total = lax.fori_loop(0, n_ba, t_sum, jnp.zeros((TB, piece), F32))
    t_lse = t_peak + jnp.log(jnp.sum(t_total, axis=1, keepdims=True))
    hi = t_lse.astype(BF16).astype(F32)
    mid = (t_lse - hi).astype(BF16).astype(F32)
    low = t_lse - hi - mid
    lane = lax.broadcasted_iota(jnp.int32, (TB, PAD), 1)
    tail = jnp.where(lane == 0, hi, jnp.where(lane == 1, mid, low)).astype(BF16)

    def t_tail(j, c):
        t_send[j, :, piece : piece + PAD] = tail
        return c

    lax.fori_loop(0, n_ba, t_tail, 0)

    def relayout(k, c):
        w_load(k).wait()
        at = pl.ds(pl.multiple_of(k * chunk, chunk), chunk)
        w_std[:, at, :] = pltpu.einshape("dir->idr", w_raw[k])
        return c

    early = 8
    lax.fori_loop(0, early, relayout, 0)

    expected = 2 * n_ba - 1 + 3 - jnp.where(t_owner == a, 1, 0)
    pl.semaphore_wait(barrier, expected)

    def t_copy(k):
        return remote(
            t_send.at[k], t_in.at[a, pl.ds(pl.multiple_of(t_slot * TB, TB), TB)],
            t_ssem.at[k], t_rsem.at[a, t_slot], t_owner, k,
        )

    def t_self(k):
        return jnp.logical_and(t_owner == a, k == b)

    def t_start(k, c):
        @pl.when(t_self(k))
        def _():
            pltpu.make_async_copy(
                t_send.at[k],
                t_in.at[a, pl.ds(pl.multiple_of(t_slot * TB, TB), TB)],
                t_rsem.at[a, t_slot],
            ).start()

        @pl.when(jnp.logical_not(t_self(k)))
        def _():
            t_copy(k).start()

        return c

    lax.fori_loop(0, n_ba, t_start, 0)

    lax.fori_loop(early, N_CHUNKS, relayout, 0)
    h_load.wait()
    for i in range(4):
        stu[:, i * piece : (i + 1) * piece] = jnp.dot(
            hid[...], w_std[i], preferred_element_type=F32
        )
    s = stu[...]
    s_peak = jnp.max(s, axis=1, keepdims=True)
    s_total = jnp.sum(jnp.exp(s - s_peak), axis=1, keepdims=True)
    s_part = s_peak + jnp.log(s_total)
    lse_buf[b] = jnp.transpose(jnp.broadcast_to(s_part, (rows, rows)))[0:1, :]

    def h_copy(step):
        to = (a + step) % 4
        return remote(
            hid_hbm.at[:, pl.ds(pl.multiple_of(to * share, share), share)],
            hall.at[pl.ds(pl.multiple_of(a * rows, rows), rows)],
            h_ssem.at[step - 1], h_rsem.at[a], to, b,
        )

    h_own = pltpu.make_async_copy(
        hid_hbm.at[:, pl.ds(pl.multiple_of(a * share, share), share)],
        hall.at[pl.ds(pl.multiple_of(a * rows, rows), rows)],
        h_rsem.at[a],
    )

    def s_copy(k):
        return remote(lse_buf.at[b], lse_buf.at[b], s_ssem.at[k], s_rsem.at[b], a, k)

    def s_start(k, c):
        @pl.when(k != b)
        def _():
            s_copy(k).start()

        return c

    lax.fori_loop(0, n_ba, s_start, 0)
    for step in range(1, 4):
        h_copy(step).start()
    h_own.start()

    def turn(k, c):
        at = pl.ds(pl.multiple_of(k * chunk, chunk), chunk)
        for i in range(4):
            w_tr[i, :, at] = jnp.transpose(w_std[i, at, :])
        return c

    lax.fori_loop(0, N_CHUNKS, turn, 0)

    def s_wait(k, c):
        @pl.when(k != b)
        def _():
            remote(lse_buf.at[k], lse_buf.at[k], s_ssem.at[k], s_rsem.at[k], a, k).wait_recv()

        return c

    lax.fori_loop(0, n_ba, s_wait, 0)
    parts = lse_buf[...]
    s_top = jnp.max(parts, axis=0)
    s_lse = s_top + jnp.log(jnp.sum(jnp.exp(parts - s_top[None]), axis=0))
    s_lse = lanes_to_rows(s_lse, rows)[:, 0:1]

    def t_wait(k, c):
        src = t_in.at[k // per_a, pl.ds(pl.multiple_of((k % per_a) * TB, TB), TB)]
        remote(t_send.at[0], src, t_ssem.at[0], t_rsem.at[k // per_a, k % per_a], a, b).wait_recv()
        return c

    lax.fori_loop(0, n_ba, t_wait, 0)
    t_parts = []
    for i in range(4):
        code = t_in[i, :, piece : piece + PAD].astype(F32)
        t_parts.append(code[:, 0:1] + code[:, 1:2] + code[:, 2:3])
    t_top = jnp.maximum(jnp.maximum(t_parts[0], t_parts[1]), jnp.maximum(t_parts[2], t_parts[3]))
    t_tot = sum(jnp.exp(v - t_top) for v in t_parts)
    t_all = t_top + jnp.log(t_tot)

    mine = pl.ds(pl.multiple_of(a * rows, rows), rows)

    def g_copy(i, src_a, to_a, ssem, rsem):
        at = pl.ds(pl.multiple_of(src_a * rows, rows), rows)
        return remote(gall.at[i, at], gall.at[i, at], ssem, rsem, to_a, b)

    def g_core(i):
        return g_copy(i, a, core_mate, g_ssem.at[0, i], g_rsem.at[0, i])

    def g_chip(i):
        return g_copy(i, a, chip_mate, g_ssem.at[1, i], g_rsem.at[1, i])

    def g_pass(i):
        return g_copy(i, chip_mate, core_mate, f_ssem.at[i], f_rsem.at[i])

    kl = jnp.zeros((rows, 128), F32)
    for i in range(4):
        log_target = t_in[i, :, 0:piece].astype(F32) - t_all
        log_student = stu[:, i * piece : (i + 1) * piece] - s_lse
        target_prob = jnp.exp(log_target)
        student_prob = jnp.exp(log_student)
        gall[i, mine, :] = (grad_scale * (student_prob - target_prob)).astype(BF16)
        term = target_prob * (log_target - log_student)
        for v in range(piece // 128):
            kl = kl + term[:, v * 128 : (v + 1) * 128]
        if i > 0:
            g_chip(i - 1).start()
            g_core(i - 1).start()
    kl_p[p] = jnp.sum(kl, axis=0, keepdims=True)
    g_chip(3).start()
    g_core(3).start()

    def r_block(q):
        return part.at[
            pl.ds(pl.multiple_of((q % per_a) * TB, TB), TB),
            pl.ds(pl.multiple_of((q // per_a) * fb_width, fb_width), fb_width),
        ]

    def r_copy(q):
        return remote(r_block(q), rs_buf.at[p], r_ssem.at[q], r_rsem.at[p], a, plane_peer(q))

    def kp_copy(q):
        return remote(kl_p.at[p], kl_p.at[p], kp_ssem.at[q], kp_rsem.at[p], a, plane_peer(q))

    r_own = pltpu.make_async_copy(r_block(p), rs_buf.at[p], r_rsem.at[p])

    def r_start(q, c):
        @pl.when(q == p)
        def _():
            r_own.start()

        @pl.when(q != p)
        def _():
            r_copy(q).start()

        return c

    def kp_start(q, c):
        @pl.when(q != p)
        def _():
            kp_copy(q).start()

        return c

    for f in range(n_fb):
        cols = slice(f * fb_width, (f + 1) * fb_width)
        total = None
        for i in range(4):
            term = jnp.dot(gall[i, mine, :], w_tr[i, :, cols], preferred_element_type=F32)
            total = term if total is None else total + term
        part[:, cols] = total.astype(BF16)
        lax.fori_loop(f * per_a, (f + 1) * per_a, r_start, 0)
    lax.fori_loop(0, plane, kp_start, 0)

    h_own.wait()
    for step in range(1, 4):
        src = (a + step) % 4
        remote(
            hid_hbm.at[:, pl.ds(0, share)],
            hall.at[pl.ds(pl.multiple_of(src * rows, rows), rows)],
            h_ssem.at[0], h_rsem.at[src], src, b,
        ).wait_recv()
    near = pl.ds(pl.multiple_of(half * 2 * rows, 2 * rows), 2 * rows)
    far = pl.ds(pl.multiple_of((1 - half) * 2 * rows, 2 * rows), 2 * rows)

    def outer(i, at):
        return lax.dot_general(
            hall[at, :], gall[i, at, :], (((0,), (0,)), ((), ())), preferred_element_type=F32
        )

    def got_core(i):
        g_copy(i, core_mate, core_mate, g_ssem.at[0, i], g_rsem.at[0, i]).wait_recv()

    def got_chip(i):
        g_copy(i, chip_mate, chip_mate, g_ssem.at[1, i], g_rsem.at[1, i]).wait_recv()
        g_pass(i).start()

    def got_pass(i):
        g_copy(i, 3 - a, core_mate, f_ssem.at[i], f_rsem.at[i]).wait_recv()

    for i in range(4):
        got_core(i)
        acc[i] = outer(i, near)
    got_chip(0)
    got_chip(1)
    got_chip(2)

    def r_wait(q, c):
        @pl.when(q == p)
        def _():
            r_own.wait()

        @pl.when(q != p)
        def _():
            remote(r_block(q), rs_buf.at[q], r_ssem.at[q], r_rsem.at[q], a, b).wait_recv()
            remote(kl_p.at[q], kl_p.at[q], kp_ssem.at[q], kp_rsem.at[q], a, b).wait_recv()

        return c

    lax.fori_loop(0, plane, r_wait, 0)

    def r_sum(q, total):
        return total + rs_buf[q].astype(F32)

    z_send[...] = lax.fori_loop(0, plane, r_sum, jnp.zeros((TB, fb_width), F32)).astype(BF16)
    kl_z[zh] = jnp.sum(kl_p[...], axis=0)
    z_copy = remote(z_send, z_recv, z_ssem, z_rsem, a, b_across)
    kz_copy = remote(kl_z.at[zh], kl_z.at[zh], kz_ssem, kz_rsem, a, b_across)
    z_copy.start()
    kz_copy.start()
    got_chip(3)
    z_copy.wait_recv()
    fin[...] = (z_send[...].astype(F32) + z_recv[...].astype(F32)).astype(BF16)
    remote(kl_z.at[1 - zh], kl_z.at[1 - zh], kz_ssem, kz_rsem, a, b_across).wait_recv()
    kl_a[a] = jnp.sum(kl_z[...], axis=0)

    def out_block(q):
        return gh_out.at[
            pl.ds(pl.multiple_of((q % per_a) * TB, TB), TB),
            pl.ds(pl.multiple_of((q // per_a) * fb_width, fb_width), fb_width),
        ]

    def a_copy(q):
        return remote(fin, out_block(p), a_ssem.at[q], a_rsem.at[p], a, plane_peer(q))

    a_own = pltpu.make_async_copy(fin, out_block(p), a_rsem.at[p])

    def a_start(q, c):
        @pl.when(q == p)
        def _():
            a_own.start()

        @pl.when(q != p)
        def _():
            a_copy(q).start()

        return c

    lax.fori_loop(0, plane, a_start, 0)

    def ka_copy(step):
        return remote(
            kl_a.at[a], kl_a.at[a], ka_ssem.at[step - 1], ka_rsem.at[a], (a + step) % 4, b
        )

    for step in range(1, 4):
        ka_copy(step).start()

    for i in range(4):
        got_pass(i)
        gw[i] = (acc[i] + outer(i, far)).astype(BF16)
    n_out = share // chunk
    gw_store = [
        pltpu.make_async_copy(w_raw.at[k], gw_out.at[pl.ds(k * chunk, chunk)], o_sem.at[k])
        for k in range(n_out)
    ]
    for k in range(n_out):
        w_raw[k] = pltpu.einshape("idr->dir", gw[:, k * chunk : (k + 1) * chunk, :])
        gw_store[k].start()

    for step in range(1, 4):
        src = (a + step) % 4
        remote(kl_a.at[src], kl_a.at[src], ka_ssem.at[0], ka_rsem.at[src], src, b).wait_recv()
    summed = jnp.sum(kl_a[...], axis=0)
    div_ref[...] = jnp.broadcast_to(
        jnp.sum(summed, axis=1, keepdims=True) / (4.0 * rows), div_ref.shape
    )

    def a_wait(q, c):
        @pl.when(q == p)
        def _():
            a_own.wait()

        @pl.when(q != p)
        def _():
            remote(fin, out_block(q), a_ssem.at[q], a_rsem.at[q], a, b).wait_recv()

        return c

    lax.fori_loop(0, plane, a_wait, 0)
    for k in range(n_out):
        gw_store[k].wait()

    def sent_ba(k, c):
        @pl.when(jnp.logical_not(t_self(k)))
        def _():
            t_copy(k).wait_send()

        @pl.when(k != b)
        def _():
            s_copy(k).wait_send()

        return c

    lax.fori_loop(0, n_ba, sent_ba, 0)

    def sent_plane(q, c):
        @pl.when(q != p)
        def _():
            r_copy(q).wait_send()
            kp_copy(q).wait_send()
            a_copy(q).wait_send()

        return c

    lax.fori_loop(0, plane, sent_plane, 0)
    for step in range(1, 4):
        h_copy(step).wait_send()
        ka_copy(step).wait_send()
    for i in range(4):
        g_core(i).wait_send()
        g_chip(i).wait_send()
        g_pass(i).wait_send()
    z_copy.wait_send()
    kz_copy.wait_send()


def on_device(n_ba, hidden, head_weight, teacher):
    rows, width = hidden.shape
    piece = head_weight.shape[3]
    share = width // 4
    plane = n_ba // 2
    per_a = n_ba // 4
    fb_width = width // (plane // per_a)
    chunk = width // N_CHUNKS
    x_size = 4 if n_ba == 32 else 1
    dma = pltpu.SemaphoreType.DMA
    out = pl.pallas_call(
        functools.partial(kernel, n_ba, x_size),
        out_shape=(
            jax.ShapeDtypeStruct((8, 128), F32),
            jax.ShapeDtypeStruct((rows, width), BF16),
            jax.ShapeDtypeStruct((share, 4, piece), BF16),
        ),
        in_specs=[pl.BlockSpec(memory_space=pl.ANY)] * 3,
        out_specs=(
            pl.BlockSpec(memory_space=pltpu.VMEM),
            pl.BlockSpec(memory_space=pl.ANY),
            pl.BlockSpec(memory_space=pl.ANY),
        ),
        scratch_shapes=[
            pltpu.VMEM((rows, width), BF16),
            pltpu.VMEM((N_CHUNKS, chunk, 4, piece), BF16),
            pltpu.VMEM((4, width, piece), BF16),
            pltpu.VMEM((4, piece, width), BF16),
            pltpu.VMEM((TB, n_ba, piece), BF16),
            pltpu.VMEM((n_ba, TB, piece + PAD), BF16),
            pltpu.VMEM((4, rows, piece + PAD), BF16),
            pltpu.VMEM((rows, 4 * piece), F32),
            pltpu.VMEM((n_ba, 1, rows), F32),
            pltpu.VMEM((4 * rows, share), BF16),
            pltpu.VMEM((4, 4 * rows, piece), BF16),
            pltpu.VMEM((4, share, piece), F32),
            pltpu.VMEM((4, share, piece), BF16),
            pltpu.VMEM((rows, width), BF16),
            pltpu.VMEM((plane, TB, fb_width), BF16),
            pltpu.VMEM((TB, fb_width), BF16),
            pltpu.VMEM((TB, fb_width), BF16),
            pltpu.VMEM((TB, fb_width), BF16),
            pltpu.VMEM((plane, 1, 128), F32),
            pltpu.VMEM((2, 1, 128), F32),
            pltpu.VMEM((4, 1, 128), F32),
            dma((2,)), dma((N_CHUNKS,)),
            dma((n_ba,)), dma((4, per_a)),
            dma((3,)), dma((4,)),
            dma((n_ba,)), dma((n_ba,)),
            dma((2, 4)), dma((2, 4)),
            dma((4,)), dma((4,)),
            dma((plane,)), dma((plane,)),
            dma, dma,
            dma((plane,)), dma((plane,)),
            dma((plane,)), dma((plane,)),
            dma, dma,
            dma((3,)), dma((4,)),
            dma((share // chunk,)),
        ],
        compiler_params=pltpu.CompilerParams(
            collective_id=0, has_side_effects=True, vmem_limit_bytes=66_000_000
        ),
    )(hidden, head_weight, teacher)
    return out[0][0, 0], out[1], out[2][:, None]


def solution(mesh):
    placed = (P("aa", None), P(None, "ba", None, None), P("ba", "aa", None, None))
    return jax.shard_map(
        functools.partial(on_device, mesh.shape["ba"]),
        mesh=mesh,
        in_specs=placed,
        out_specs=(P(), P("aa", None), P("aa", "ba", None, None)),
        check_vma=False,
    )
```

time: 546 us -> 66.9 us (0.12)
  blocking collectives: 448 us -> 0 us
  Pallas kernels: 0 us -> 57.7 us
  matrix products: 25.6 us -> 0 us
  local copies, waits for them, and re-layouts: 26.7 us -> 7.88 us
  between operations: 15.9 us -> 0.64 us
  starting transfers between devices: 14.3 us -> 0 us
  other arithmetic: 11.8 us -> 0 us
    psum x3 -> x0, blocking collectives: 351 us -> none  [the longest x1 200 us: on_device(): grad_hidden = lax.psum(partial_hidden, 'ba').astype(jnp.bfloat16)]
    pmax x1 -> x0, blocking collectives: 97.3 us -> none  [on_device(): student_peak, target_peak = lax.pmax((student_peak, target_peak), 'ba')]
    pallas_call x0 -> x1, Pallas kernels: none -> 57.7 us  [on_device(): pl.pallas_call(functools.partial(kernel, n_ba, x_size), out_shape=(jax.Sh...]
    dot_general x3 -> x0, matrix products: 25.6 us -> none  [the longest x1 10.1 us: on_device(): lax.dot_general(hidden, gradient, (((0,), (0,)), ((), ())), preferred_ele...]
    unnamed x10 -> x2, local copies, waits for them, and re-layouts: 24.3 us -> 6.69 us
    all_to_all x2 -> x0, starting transfers between devices: 14.2 us -> none  [the longest x1 10.7 us: on_device(): lax.all_to_all(teacher, 'ba', split_axis=2, concat_axis=0, tiled=True)]
    convert_element_type x3 -> x0, other arithmetic: 8.5 us -> none  [the longest x1 4.76 us: on_device(): grad_flat.astype(jnp.bfloat16)]
  transfers between devices with their start and end apart: 3 -> 0, of which waited for: 2 -> 0; matrix products, arithmetic and copies ran while one was open for 5% -> 0% of each run, Pallas kernels for 0% -> 0%
where the time goes in v1:
time: 66.9 us; the launch traced here: 66.2 us
  Pallas kernels  57.7 us (86%)
  local copies, waits for them, and re-layouts  7.88 us (12%)
    pallas_call x1, Pallas kernels, on_device(): pl.pallas_call(functools.partial(kernel, n_ba, x_size), out_shape=(jax.Sh...  57.7 us
    unnamed x2, local copies, waits for them, and re-layouts  6.69 us

profile of v1, /device:TPU:0, one launch (start us, length us, event | category | flops | bytes accessed | tf_op | source)
XLA Modules:
  0.0 66.2 jit_solution(74722735772730627)
XLA Ops:
  0.6 57.7 %shard_map.58 = (f32[8,128]{1,0:T(8,128)}, bf16[128,3072]{1,0:T(8,128)(2,1)}, bf16[768,4,512]{2,1,0:T(4,128)(2,1)}) custom-call(bf16[128,3072]{1,0:T(8,128)(2,1)} %hid_hbm.1, bf16[3072,1,4,512]{3,2,1,0:T(4,128)(2,1)} %w_hbm.1, bf16[16,1,32,512]{3,2,1,0:T(8,128)(2,1)} %t_hbm.1), custom_call_target="tpu_custom_call" | custom-call | tf_op jit(solution)/shard_map/pallas_call | solution.py:485
  58.3 1.2 %slice.3 = f32[1,1]{1,0:T(1,128)} slice(f32[8,128]{1,0:T(8,128)} %get-tuple-element.6), slice={[0:1], [0:1]} | slice | bytes 8 | tf_op jit(solution)/shard_map/slice | solution.py:538
  59.5 2.1 %copy.9 = bf16[128,3072]{1,0:T(8,128)(2,1)} copy(bf16[128,3072]{1,0:T(8,128)(2,1)} %get-tuple-element.16) | data formatting | bytes 1572864
  61.6 4.6 %copy.10 = bf16[768,1,4,512]{3,2,1,0:T(4,128)(2,1)} copy(bf16[768,1,4,512]{3,2,1,0:T(4,128)(2,1)} %bitcast.4) | data formatting | bytes 6291456

commit v2 on v0

v2 whole, which is shorter than its diff:
```python
import functools

import jax
import jax.numpy as jnp
from jax import lax
from jax.experimental import pallas as pl
from jax.experimental.pallas import tpu as pltpu
from jax.sharding import PartitionSpec as P

MESH = pl.DeviceIdType.MESH
F32 = jnp.float32
BF16 = jnp.bfloat16
grad_scale = 256.0
N_CHUNKS = 6
STORES = 6
VMEM_LIMIT = 58_000_000
TB = 16
HALVES = 2


def finish(pending):
    for wait in pending:
        wait()


def lanes_to_rows(row, n):
    return jnp.transpose(jnp.broadcast_to(row, (n, n)))


def kernel(
    n_ba, x_size,
    hid_hbm, w_hbm, t_hbm,
    div_ref, gh_out, gw_out,
    hid, w_raw, w_std, w_tr, t_raw, t_send, t_in, stu, lse_buf, n_send, n_in,
    hall, gall, acc, part, rs_buf, z_send, z_recv, fin, kl_p, kl_z, kl_a,
    in_sem, w_sem, t_ssem, t_rsem, n_ssem, n_rsem, h_ssem, h_rsem, s_ssem, s_rsem,
    g_ssem, g_rsem, r_ssem, r_rsem, z_ssem, z_rsem, a_ssem, a_rsem,
    kp_ssem, kp_rsem, kz_ssem, kz_rsem, ka_ssem, ka_rsem,
):
    a = lax.axis_index("aa")
    b = lax.axis_index("ba")
    width = hid.shape[1]
    rows = hid.shape[0]
    piece = w_raw.shape[3]
    per_a = n_ba // 4
    plane = n_ba // 2
    share = width // 4
    n_fb = plane // per_a
    fb_width = width // n_fb // HALVES
    chunk = w_raw.shape[1]
    t_owner = b // per_a
    t_slot = b % per_a
    zh = (b // x_size) % 2
    p = (b // (2 * x_size)) * x_size + b % x_size
    half = a // 2

    def plane_peer(q):
        return ((q // x_size) * 2 + zh) * x_size + q % x_size

    b_across = plane_peer(p) + (1 - 2 * zh) * x_size
    core_mate = a + 1 - 2 * (a % 2)
    chip_mate = (a + 2) % 4

    def remote(src, dst, ssem, rsem, to_a, to_b):
        return pltpu.make_async_remote_copy(
            src_ref=src, dst_ref=dst, send_sem=ssem, recv_sem=rsem,
            device_id=(to_a, to_b), device_id_type=MESH,
        )

    pending = []

    def drain(sem, like):
        pending.append(remote(like, like, sem, sem, a, b).wait_send)

    def drain_t(sem, ref):
        def wait():
            @pl.when(t_owner == a)
            def _():
                remote(ref.at[: n_ba - 1], ref.at[: n_ba - 1], sem, sem, a, b).wait_send()

            @pl.when(t_owner != a)
            def _():
                remote(ref, ref, sem, sem, a, b).wait_send()

        pending.append(wait)

    t_load = pltpu.make_async_copy(t_hbm.at[:, 0], t_raw, in_sem.at[0])
    h_load = pltpu.make_async_copy(hid_hbm, hid, in_sem.at[1])
    t_load.start()

    def w_load(k):
        return pltpu.make_async_copy(
            w_hbm.at[pl.ds(k * chunk, chunk), 0], w_raw.at[k], w_sem.at[k]
        )

    h_load.start()
    for k in range(N_CHUNKS):
        w_load(k).start()

    barrier = pltpu.get_barrier_semaphore()

    def greet(to_a, to_b):
        pl.semaphore_signal(barrier, inc=1, device_id=(to_a, to_b), device_id_type=MESH)

    for step in range(n_ba):
        src_a, src_b = (a + step // per_a) % 4, a * per_a + (b + step) % per_a
        if step:
            greet(src_a, src_b)
        else:

            @pl.when(t_owner != a)
            def _():
                greet(src_a, src_b)

    for step in range(1, n_ba):
        greet(a, (b + step) % n_ba)
    for step in range(1, 4):
        greet((a + step) % 4, b)

    t_load.wait()
    t_send[...] = pltpu.einshape("tjr->jtr", t_raw[...])
    expected = 2 * n_ba - 1 + 3 - jnp.where(t_owner == a, 1, 0)
    pl.semaphore_wait(barrier, expected)
    t_dst = t_in.at[a, pl.ds(pl.multiple_of(t_slot * TB, TB), TB)]

    def to_owner(src_of, dst, ssem, rsem):
        for step in range(n_ba):
            k = (b + step) % n_ba
            copy = remote(src_of(k), dst, ssem, rsem, t_owner, k)
            if step:
                copy.start()
            else:

                @pl.when(t_owner != a)
                def _():
                    copy.start()

                @pl.when(t_owner == a)
                def _():
                    pltpu.make_async_copy(src_of(k), dst, rsem).start()

    to_owner(lambda k: t_send.at[k], t_dst, t_ssem, t_rsem)
    drain_t(t_ssem, t_send)

    def t_max(j, m):
        return jnp.maximum(m, t_send[j].astype(F32))

    t_peak = lax.fori_loop(1, n_ba, t_max, t_send[0].astype(F32))
    t_peak = jnp.max(t_peak, axis=1, keepdims=True)

    def t_sum(j, s):
        return s + jnp.exp(t_send[j].astype(F32) - t_peak)

    t_total = lax.fori_loop(0, n_ba, t_sum, jnp.zeros((TB, piece), F32))
    t_lse = t_peak + jnp.log(jnp.sum(t_total, axis=1, keepdims=True))
    token = lax.broadcasted_iota(jnp.int32, (TB, rows), 0)
    lane = lax.broadcasted_iota(jnp.int32, (TB, rows), 1)
    n_send[...] = jnp.sum(
        jnp.where(lane == token + t_slot * TB, t_lse, 0.0), axis=0, keepdims=True
    )

    to_owner(lambda k: n_send, n_in.at[a, t_slot], n_ssem, n_rsem)
    drain_t(n_ssem, lse_buf)

    sub = chunk // 2

    def relayout(k, c):
        at = pl.ds(pl.multiple_of(k * sub, sub), sub)
        w_std[:, at, :] = pltpu.einshape(
            "dir->idr", w_raw[k // 2, pl.ds(pl.multiple_of((k % 2) * sub, sub), sub)]
        )
        return c

    h_load.wait()
    for part_of in range(2):
        for k in range(part_of * N_CHUNKS // 2, (part_of + 1) * N_CHUNKS // 2):
            w_load(k).wait()
            lax.fori_loop(2 * k, 2 * k + 2, relayout, 0)
        deep = slice(part_of * width // 2, (part_of + 1) * width // 2)
        for i in range(4):
            at = slice(i * piece, (i + 1) * piece)
            product = jnp.dot(hid[:, deep], w_std[i, deep], preferred_element_type=F32)
            stu[:, at] = product if part_of == 0 else stu[:, at] + product
    s = stu[...]
    s_peak = jnp.max(s, axis=1, keepdims=True)
    s_total = jnp.sum(jnp.exp(s - s_peak), axis=1, keepdims=True)
    s_part = s_peak + jnp.log(s_total)
    lse_buf[b] = jnp.transpose(jnp.broadcast_to(s_part, (rows, rows)))[0:1, :]

    for step in range(1, n_ba):
        remote(lse_buf.at[b], lse_buf.at[b], s_ssem, s_rsem, a, (b + step) % n_ba).start()
    drain(s_ssem, lse_buf.at[: n_ba - 1])

    mine = pl.ds(pl.multiple_of(a * rows, rows), rows)

    def h_cols(to):
        return hid_hbm.at[:, pl.ds(pl.multiple_of(to * share, share), share)]

    for step in range(1, 4):
        to = (a + step) % 4
        remote(h_cols(to), hall.at[mine], h_ssem, h_rsem, to, b).start()
    pltpu.make_async_copy(h_cols(a), hall.at[mine], h_rsem).start()
    drain(h_ssem, hall.at[: 3 * rows])

    def turn(k, c):
        at = pl.ds(pl.multiple_of(k * sub, sub), sub)
        for i in range(4):
            w_tr[i, :, at] = jnp.transpose(w_std[i, at, :])
        return c

    lax.fori_loop(0, 2 * N_CHUNKS, turn, 0)

    def arrived(sem, like):
        remote(like, like, sem, sem, a, b).wait_recv()

    arrived(s_rsem, lse_buf.at[: n_ba - 1])
    parts = lse_buf[...]
    s_top = jnp.max(parts, axis=0)
    s_lse = s_top + jnp.log(jnp.sum(jnp.exp(parts - s_top[None]), axis=0))
    s_lse = lanes_to_rows(s_lse, rows)[:, 0:1]

    arrived(t_rsem, t_in)
    arrived(n_rsem, n_in)
    t_parts = jnp.sum(n_in[...], axis=1)
    t_top = jnp.max(t_parts, axis=0)
    t_all = t_top + jnp.log(jnp.sum(jnp.exp(t_parts - t_top[None]), axis=0))
    t_all = lanes_to_rows(t_all, rows)[:, 0:1]

    def g_copy(i, src_a, to_a, ssem, rsem):
        at = pl.ds(pl.multiple_of(src_a * rows, rows), rows)
        return remote(gall.at[i, at], gall.at[i, at], ssem, rsem, to_a, b)

    def g_core(i):
        return g_copy(i, a, core_mate, g_ssem.at[0], g_rsem.at[0, i])

    def g_chip(i):
        return g_copy(i, a, chip_mate, g_ssem.at[1], g_rsem.at[1, i])

    def g_pass(i):
        return g_copy(i, chip_mate, core_mate, g_ssem.at[2], g_rsem.at[2, i])

    for k in range(3):
        drain(g_ssem.at[k], gall.at[:, mine])

    kl = jnp.zeros((rows, 128), F32)
    for i in range(4):
        log_target = t_in[i].astype(F32) - t_all
        log_student = stu[:, i * piece : (i + 1) * piece] - s_lse
        target_prob = jnp.exp(log_target)
        student_prob = jnp.exp(log_student)
        gall[i, mine, :] = (grad_scale * (student_prob - target_prob)).astype(BF16)
        term = target_prob * (log_target - log_student)
        for v in range(piece // 128):
            kl = kl + term[:, v * 128 : (v + 1) * 128]
        if i > 0:
            g_chip(i - 1).start()
            g_core(i - 1).start()
    kl_p[p] = jnp.sum(kl, axis=0, keepdims=True)
    g_core(3).start()

    def block_of(ref, q, f):
        return ref.at[
            pl.ds(pl.multiple_of((q % per_a) * TB, TB), TB),
            pl.ds(pl.multiple_of((f * n_fb + q // per_a) * fb_width, fb_width), fb_width),
        ]

    def to_plane(src_of, dst, ssem, rsem):
        for step in range(1, plane):
            q = (p + step) % plane
            remote(src_of(q), dst, ssem, rsem, a, plane_peer(q)).start()

    for f in range(HALVES):
        cols = slice(f * n_fb * fb_width, (f + 1) * n_fb * fb_width)
        total = None
        for i in range(4):
            term = jnp.dot(gall[i, mine, :], w_tr[i, :, cols], preferred_element_type=F32)
            total = term if total is None else total + term
        part[:, cols] = total.astype(BF16)
        to_plane(lambda q: block_of(part, q, f), rs_buf.at[f, p], r_ssem.at[f], r_rsem.at[f])
        pltpu.make_async_copy(block_of(part, p, f), rs_buf.at[f, p], r_rsem.at[f]).start()
        drain(r_ssem.at[f], rs_buf.at[f, : plane - 1])
    to_plane(lambda q: kl_p.at[p], kl_p.at[p], kp_ssem, kp_rsem)
    drain(kp_ssem, kl_p.at[: plane - 1])

    arrived(h_rsem, hall)
    near = pl.ds(pl.multiple_of(half * 2 * rows, 2 * rows), 2 * rows)
    far = pl.ds(pl.multiple_of((1 - half) * 2 * rows, 2 * rows), 2 * rows)

    def outer(i, at):
        return lax.dot_general(
            hall[at, :], gall[i, at, :], (((0,), (0,)), ((), ())), preferred_element_type=F32
        )

    def got_core(i):
        arrived(g_rsem.at[0, i], gall.at[i, mine])

    def got_chip(i):
        arrived(g_rsem.at[1, i], gall.at[i, mine])
        g_pass(i).start()

    def got_pass(i):
        arrived(g_rsem.at[2, i], gall.at[i, mine])

    for i in range(4):
        got_core(i)
        acc[i] = outer(i, near)
    got_chip(0)
    got_chip(1)

    def r_sums(f):
        arrived(r_rsem.at[f], rs_buf.at[f])

        def add(q, total):
            return total + rs_buf[f, q].astype(F32)

        total = lax.fori_loop(0, plane, add, jnp.zeros((TB, fb_width), F32))
        z_send[f] = total.astype(BF16)
        z_copy(f).start()
        drain(z_ssem.at[f], z_send.at[f])

    def z_copy(f):
        return remote(z_send.at[f], z_recv.at[f], z_ssem.at[f], z_rsem.at[f], a, b_across)

    def spread(f):
        z_copy(f).wait_recv()
        fin[f] = (z_send[f].astype(F32) + z_recv[f].astype(F32)).astype(BF16)
        to_plane(lambda q: fin.at[f], block_of(gh_out, p, f), a_ssem.at[f], a_rsem.at[f])
        pltpu.make_async_copy(fin.at[f], block_of(gh_out, p, f), a_rsem.at[f]).start()
        drain(a_ssem.at[f], rs_buf.at[f, : plane - 1])

    r_sums(0)
    g_chip(3).start()
    got_chip(2)
    spread(0)
    r_sums(1)

    arrived(kp_rsem, kl_p.at[: plane - 1])
    kl_z[zh] = jnp.sum(kl_p[...], axis=0)
    kz_copy = remote(kl_z.at[zh], kl_z.at[zh], kz_ssem, kz_rsem, a, b_across)
    kz_copy.start()
    drain(kz_ssem, kl_z.at[zh])
    got_chip(3)
    spread(1)
    remote(kl_z.at[1 - zh], kl_z.at[1 - zh], kz_ssem, kz_rsem, a, b_across).wait_recv()
    kl_a[a] = jnp.sum(kl_z[...], axis=0)

    for step in range(1, 4):
        remote(kl_a.at[a], kl_a.at[a], ka_ssem, ka_rsem, (a + step) % 4, b).start()
    drain(ka_ssem, kl_a.at[:3])

    for i in range(4):
        got_pass(i)
        w_std[i, 0:share, :] = (acc[i] + outer(i, far)).astype(BF16)
    for k in range(share // sub):
        at = slice(k * sub, (k + 1) * sub)
        gw_out[at] = pltpu.einshape("idr->dir", w_std[:, at, :])
    arrived(ka_rsem, kl_a.at[:3])
    summed = jnp.sum(kl_a[...], axis=0)
    div_ref[...] = jnp.broadcast_to(
        jnp.sum(summed, axis=1, keepdims=True) / (4.0 * rows), div_ref.shape
    )
    half_width = width // HALVES
    for f in range(HALVES):
        arrived(a_rsem.at[f], gh_out.at[:, f * half_width : (f + 1) * half_width])
    finish(pending)


def store(div_in, gh_in, gw_in, div_ref, gh_hbm, gw_hbm, sem):
    n = gw_in.shape[0] // STORES
    copies = [
        pltpu.make_async_copy(
            gw_in.at[pl.ds(k * n, n)], gw_hbm.at[pl.ds(k * n, n)], sem.at[k]
        )
        for k in range(STORES)
    ]
    copies.append(pltpu.make_async_copy(gh_in, gh_hbm, sem.at[STORES]))
    for copy in copies:
        copy.start()
    div_ref[...] = div_in[0:1, 0:1]
    for copy in copies:
        copy.wait()


def on_device(n_ba, hidden, head_weight, teacher):
    rows, width = hidden.shape
    piece = head_weight.shape[3]
    share = width // 4
    plane = n_ba // 2
    per_a = n_ba // 4
    fb_width = width // (plane // per_a) // HALVES
    chunk = width // N_CHUNKS
    x_size = 4 if n_ba == 32 else 1
    dma = pltpu.SemaphoreType.DMA
    vmem, anywhere = pltpu.VMEM, pl.BlockSpec(memory_space=pl.ANY)
    results = pl.pallas_call(
        functools.partial(kernel, n_ba, x_size),
        out_shape=(
            vmem((8, 128), F32),
            vmem((rows, width), BF16),
            vmem((share, 4, piece), BF16),
        ),
        in_specs=[anywhere] * 3,
        out_specs=(pl.BlockSpec(memory_space=vmem),) * 3,
        scratch_shapes=[
            vmem((rows, width), BF16),
            vmem((N_CHUNKS, chunk, 4, piece), BF16),
            vmem((4, width, piece), BF16),
            vmem((4, piece, width), BF16),
            vmem((TB, n_ba, piece), BF16),
            vmem((n_ba, TB, piece), BF16),
            vmem((4, rows, piece), BF16),
            vmem((rows, 4 * piece), F32),
            vmem((n_ba, 1, rows), F32),
            vmem((1, rows), F32),
            vmem((4, per_a, 1, rows), F32),
            vmem((4 * rows, share), BF16),
            vmem((4, 4 * rows, piece), BF16),
            vmem((4, share, piece), F32),
            vmem((rows, width), BF16),
            vmem((HALVES, plane, TB, fb_width), BF16),
            vmem((HALVES, TB, fb_width), BF16),
            vmem((HALVES, TB, fb_width), BF16),
            vmem((HALVES, TB, fb_width), BF16),
            vmem((plane, 1, 128), F32),
            vmem((2, 1, 128), F32),
            vmem((4, 1, 128), F32),
            dma((2,)), dma((N_CHUNKS,)),
            dma, dma,
            dma, dma,
            dma, dma,
            dma, dma,
            dma((3,)), dma((3, 4)),
            dma((HALVES,)), dma((HALVES,)),
            dma((HALVES,)), dma((HALVES,)),
            dma((HALVES,)), dma((HALVES,)),
            dma, dma,
            dma, dma,
            dma, dma,
        ],
        compiler_params=pltpu.CompilerParams(
            collective_id=0, has_side_effects=True, vmem_limit_bytes=VMEM_LIMIT
        ),
    )(hidden, head_weight, teacher)
    div, grad_hidden, grad_head = pl.pallas_call(
        store,
        out_shape=(
            jax.ShapeDtypeStruct((1, 1), F32),
            jax.ShapeDtypeStruct((rows, width), BF16),
            jax.ShapeDtypeStruct((share, 4, piece), BF16),
        ),
        in_specs=[pl.BlockSpec(memory_space=vmem)] * 3,
        out_specs=(pl.BlockSpec(memory_space=vmem), anywhere, anywhere),
        scratch_shapes=[dma((STORES + 1,))],
        compiler_params=pltpu.CompilerParams(vmem_limit_bytes=1_000_000),
    )(*(pltpu.with_memory_space_constraint(x, vmem) for x in results))
    return div.reshape(()), grad_hidden, grad_head[:, None]


def solution(mesh):
    placed = (P("aa", None), P(None, "ba", None, None), P("ba", "aa", None, None))
    return jax.shard_map(
        functools.partial(on_device, mesh.shape["ba"]),
        mesh=mesh,
        in_specs=placed,
        out_specs=(P(), P("aa", None), P("aa", "ba", None, None)),
        check_vma=False,
    )
```

time: 546 us -> 51.2 us (0.09)
  blocking collectives: 448 us -> 0 us
  Pallas kernels: 0 us -> 50 us
  local copies, waits for them, and re-layouts: 26.7 us -> 0 us
  matrix products: 25.6 us -> 0 us
  between operations: 15.9 us -> 0.64 us
  starting transfers between devices: 14.3 us -> 0 us
  other arithmetic: 11.8 us -> 0 us
    psum x3 -> x0, blocking collectives: 351 us -> none  [the longest x1 200 us: on_device(): grad_hidden = lax.psum(partial_hidden, 'ba').astype(jnp.bfloat16)]
    pmax x1 -> x0, blocking collectives: 97.3 us -> none  [on_device(): student_peak, target_peak = lax.pmax((student_peak, target_peak), 'ba')]
    pallas_call x0 -> x2, Pallas kernels: none -> 50 us  [the longest x1 47.5 us: on_device(): pl.pallas_call(functools.partial(kernel, n_ba, x_size), out_shape=(vmem((...]
    dot_general x3 -> x0, matrix products: 25.6 us -> none  [the longest x1 10.1 us: on_device(): lax.dot_general(hidden, gradient, (((0,), (0,)), ((), ())), preferred_ele...]
    unnamed x10 -> x0, local copies, waits for them, and re-layouts: 24.3 us -> none
    all_to_all x2 -> x0, starting transfers between devices: 14.2 us -> none  [the longest x1 10.7 us: on_device(): lax.all_to_all(teacher, 'ba', split_axis=2, concat_axis=0, tiled=True)]
    convert_element_type x3 -> x0, other arithmetic: 8.5 us -> none  [the longest x1 4.76 us: on_device(): grad_flat.astype(jnp.bfloat16)]
  transfers between devices with their start and end apart: 3 -> 0, of which waited for: 2 -> 0; matrix products, arithmetic and copies ran while one was open for 5% -> 0% of each run, Pallas kernels for 0% -> 0%
where the time goes in v2:
time: 51.2 us; the launch traced here: 50.6 us
  Pallas kernels  50 us (98%)
  between operations  0.64 us (1%)
    pallas_call x1, Pallas kernels, on_device(): pl.pallas_call(functools.partial(kernel, n_ba, x_size), out_shape=(vmem((...  47.5 us
    pallas_call x1, Pallas kernels, on_device(): pl.pallas_call(store, out_shape=(jax.ShapeDtypeStruct((1, 1), F32), jax.S...  2.49 us

profile of v2, /device:TPU:0, one launch (start us, length us, event | category | flops | bytes accessed | tf_op | source)
XLA Modules:
  0.0 50.6 jit_solution(4051359840644885784)
XLA Ops:
  0.6 47.5 %shard_map.58 = (f32[8,128]{1,0:T(8,128)S(1)}, bf16[128,3072]{1,0:T(8,128)(2,1)S(1)}, bf16[768,4,512]{2,1,0:T(4,128)(2,1)S(1)}) custom-call(bf16[128,3072]{1,0:T(8,128)(2,1)} %hid_hbm.1, bf16[3072,1,4,512]{3,2,1,0:T(4,128)(2,1)} %w_hbm.1, bf16[16,1,32,512]{3,2,1,0:T(8,128)(2,1)} %t_hbm.1), custom_call_target="tpu_custom_call" | custom-call | tf_op jit(solution)/shard_map/pallas_call | solution.py:395
  48.2 2.5 %shard_map.59 = (f32[1,1]{1,0:T(1,128)}, bf16[128,3072]{1,0:T(8,128)(2,1)}, bf16[768,4,512]{2,1,0:T(4,128)(2,1)}) custom-call(f32[8,128]{1,0:T(8,128)S(1)} %get-tuple-element.9.div_in, bf16[128,3072]{1,0:T(8,128)(2,1)S(1)} %get-tuple-element.10.gh_in, bf16[768,4,512]{2,1,0:T(4,128)(2,1)S(1)} %get-tuple-element.11.gw_in), custom_call_target="tpu_custom_call" | custom-call | tf_op jit(solution)/shard_map/pallas_call | solution.py:444

commit v3 on v2

--- a/solution.py
+++ b/solution.py
@@ -13,14 +13,30 @@
 grad_scale = 256.0
 N_CHUNKS = 6
 STORES = 6
+HIDDEN_AT = 6
+AHEAD = 3
+LOADS_AFTER = 36
+DIRECT = 2
+TALK_AT = 1
+ORDER = "c0,r0,h0,h1,h2,c1,r1,h3,s0,h4,h5"
+ORDER_TAIL = "r2,p0,h6,s1,h7,m0,s2,q0,m1,c2,m2,c3,m3"
 VMEM_LIMIT = 58_000_000
 TB = 16
-HALVES = 2
+HALVES = 3
 
 
 def finish(pending):
     for wait in pending:
         wait()
+
+
+def ring(d, n):
+    return min(d, n - d)
+
+
+def offsets(y_size, x_size):
+    steps = [(y, z, x) for y in range(y_size) for z in range(2) for x in range(x_size)]
+    return sorted(steps, key=lambda s: -(ring(s[0], y_size) + 2 * s[1] + ring(s[2], x_size)))
 
 
 def lanes_to_rows(row, n):
@@ -50,8 +66,16 @@
     chunk = w_raw.shape[1]
     t_owner = b // per_a
     t_slot = b % per_a
-    zh = (b // x_size) % 2
-    p = (b // (2 * x_size)) * x_size + b % x_size
+    y_size = n_ba // (2 * x_size)
+    yy, zh, xx = b // (2 * x_size), (b // x_size) % 2, b % x_size
+    p = yy * x_size + xx
+    steps = offsets(y_size, x_size)
+    plane_steps = [s for s in steps if s[1] == 0]
+
+    def moved(step):
+        y, z, x = step
+        return (((yy + y) % y_size) * 2 + (zh + z) % 2) * x_size + (xx + x) % x_size
+
     half = a // 2
 
     def plane_peer(q):
@@ -93,18 +117,38 @@
             w_hbm.at[pl.ds(k * chunk, chunk), 0], w_raw.at[k], w_sem.at[k]
         )
 
-    h_load.start()
-    for k in range(N_CHUNKS):
-        w_load(k).start()
-
     barrier = pltpu.get_barrier_semaphore()
 
     def greet(to_a, to_b):
         pl.semaphore_signal(barrier, inc=1, device_id=(to_a, to_b), device_id_type=MESH)
 
-    for step in range(n_ba):
-        src_a, src_b = (a + step // per_a) % 4, a * per_a + (b + step) % per_a
-        if step:
+    greetings = []
+    for step in steps:
+        hops = ring(step[0], y_size) + 2 * step[1] + ring(step[2], x_size)
+        if hops:
+            greetings.append((hops, 0, step))
+    for da in range(4):
+        for step in steps:
+            if step[0] == 0:
+                hops = ring(step[2], x_size) + (1 if da // 2 else 2 * step[1]) + 1
+                greetings.append((hops, 1 + da, step))
+    greetings.sort(key=lambda g: -g[0])
+
+    def start_loads():
+        h_load.start()
+        for k in range(AHEAD):
+            w_load(k).start()
+
+    for n, (_, kind, step) in enumerate(greetings):
+        if n == LOADS_AFTER:
+            start_loads()
+        if kind == 0:
+            greet(a, moved(step))
+            continue
+        da = kind - 1
+        src_a = ((half + da // 2) % 2) * 2 + (a + da) % 2
+        src_b = (a * 2 + (zh + step[1]) % 2) * x_size + (xx + step[2]) % x_size
+        if da or step != (0, 0, 0):
             greet(src_a, src_b)
         else:
 
@@ -112,36 +156,14 @@
             def _():
                 greet(src_a, src_b)
 
-    for step in range(1, n_ba):
-        greet(a, (b + step) % n_ba)
+    b_near = moved((0, 1, 0))
     for step in range(1, 4):
         greet((a + step) % 4, b)
+    for to_a in (chip_mate, 3 - a):
+        greet(to_a, b_near)
 
     t_load.wait()
     t_send[...] = pltpu.einshape("tjr->jtr", t_raw[...])
-    expected = 2 * n_ba - 1 + 3 - jnp.where(t_owner == a, 1, 0)
-    pl.semaphore_wait(barrier, expected)
-    t_dst = t_in.at[a, pl.ds(pl.multiple_of(t_slot * TB, TB), TB)]
-
-    def to_owner(src_of, dst, ssem, rsem):
-        for step in range(n_ba):
-            k = (b + step) % n_ba
-            copy = remote(src_of(k), dst, ssem, rsem, t_owner, k)
-            if step:
-                copy.start()
-            else:
-
-                @pl.when(t_owner != a)
-                def _():
-                    copy.start()
-
-                @pl.when(t_owner == a)
-                def _():
-                    pltpu.make_async_copy(src_of(k), dst, rsem).start()
-
-    to_owner(lambda k: t_send.at[k], t_dst, t_ssem, t_rsem)
-    drain_t(t_ssem, t_send)
-
     def t_max(j, m):
         return jnp.maximum(m, t_send[j].astype(F32))
 
@@ -159,9 +181,6 @@
         jnp.where(lane == token + t_slot * TB, t_lse, 0.0), axis=0, keepdims=True
     )
 
-    to_owner(lambda k: n_send, n_in.at[a, t_slot], n_ssem, n_rsem)
-    drain_t(n_ssem, lse_buf)
-
     sub = chunk // 2
 
     def relayout(k, c):
@@ -171,10 +190,41 @@
         )
         return c
 
+    t_dst = t_in.at[a, pl.ds(pl.multiple_of(t_slot * TB, TB), TB)]
+
+    def to_owner(src_of, dst, ssem, rsem):
+        for step in steps:
+            k = moved(step)
+            copy = remote(src_of(k), dst, ssem, rsem, t_owner, k)
+            if step != (0, 0, 0):
+                copy.start()
+            else:
+
+                @pl.when(t_owner != a)
+                def _():
+                    copy.start()
+
+                @pl.when(t_owner == a)
+                def _():
+                    pltpu.make_async_copy(src_of(k), dst, rsem).start()
+
+    def talk():
+        expected = 2 * n_ba - 1 + 5 - jnp.where(t_owner == a, 1, 0)
+        pl.semaphore_wait(barrier, expected)
+        to_owner(lambda k: t_send.at[k], t_dst, t_ssem, t_rsem)
+        to_owner(lambda k: n_send, n_in.at[a, t_slot], n_ssem, n_rsem)
+
+    drain_t(t_ssem, t_send)
+    drain_t(n_ssem, lse_buf)
+    pl.when(zh != 0)(talk)
     h_load.wait()
     for part_of in range(2):
+        if part_of == TALK_AT:
+            pl.when(zh == 0)(talk)
         for k in range(part_of * N_CHUNKS // 2, (part_of + 1) * N_CHUNKS // 2):
             w_load(k).wait()
+            if k + AHEAD < N_CHUNKS:
+                w_load(k + AHEAD).start()
             lax.fori_loop(2 * k, 2 * k + 2, relayout, 0)
         deep = slice(part_of * width // 2, (part_of + 1) * width // 2)
         for i in range(4):
@@ -187,19 +237,25 @@
     s_part = s_peak + jnp.log(s_total)
     lse_buf[b] = jnp.transpose(jnp.broadcast_to(s_part, (rows, rows)))[0:1, :]
 
-    for step in range(1, n_ba):
-        remote(lse_buf.at[b], lse_buf.at[b], s_ssem, s_rsem, a, (b + step) % n_ba).start()
+    for step in steps[:-1]:
+        remote(lse_buf.at[b], lse_buf.at[b], s_ssem, s_rsem, a, moved(step)).start()
     drain(s_ssem, lse_buf.at[: n_ba - 1])
 
     mine = pl.ds(pl.multiple_of(a * rows, rows), rows)
 
-    def h_cols(to):
-        return hid_hbm.at[:, pl.ds(pl.multiple_of(to * share, share), share)]
-
-    for step in range(1, 4):
-        to = (a + step) % 4
-        remote(h_cols(to), hall.at[mine], h_ssem, h_rsem, to, b).start()
-    pltpu.make_async_copy(h_cols(a), hall.at[mine], h_rsem).start()
+    def h_part(to_a, to_b, start, size):
+        src = hid_hbm.at[pl.ds(start, size), pl.ds(pl.multiple_of(to_a * share, share), share)]
+        dst = hall.at[pl.ds(pl.multiple_of(a * rows + start, size), size)]
+        return remote(src, dst, h_ssem, h_rsem, to_a, to_b)
+
+    def send_hidden():
+        for to_a in (chip_mate, 3 - a):
+            h_part(to_a, b, 0, rows // 2).start()
+            h_part(to_a, b_near, rows // 2, rows // 2).start()
+        h_part(core_mate, b, 0, rows).start()
+        own = hid_hbm.at[:, pl.ds(pl.multiple_of(a * share, share), share)]
+        pltpu.make_async_copy(own, hall.at[mine], h_rsem).start()
+
     drain(h_ssem, hall.at[: 3 * rows])
 
     def turn(k, c):
@@ -208,7 +264,9 @@
             w_tr[i, :, at] = jnp.transpose(w_std[i, at, :])
         return c
 
-    lax.fori_loop(0, 2 * N_CHUNKS, turn, 0)
+    lax.fori_loop(0, HIDDEN_AT, turn, 0)
+    send_hidden()
+    lax.fori_loop(HIDDEN_AT, 2 * N_CHUNKS, turn, 0)
 
     def arrived(sem, like):
         remote(like, like, sem, sem, a, b).wait_recv()
@@ -235,6 +293,11 @@
 
     def g_chip(i):
         return g_copy(i, a, chip_mate, g_ssem.at[1], g_rsem.at[1, i])
+
+    def g_late(n):
+        i, k = DIRECT + n // 4, n % 4
+        at = pl.ds(pl.multiple_of(a * rows + k * (rows // 4), rows // 4), rows // 4)
+        remote(gall.at[i, at], gall.at[i, at], g_ssem.at[1], g_rsem.at[1, i], chip_mate, b).start()
 
     def g_pass(i):
         return g_copy(i, chip_mate, core_mate, g_ssem.at[2], g_rsem.at[2, i])
@@ -253,7 +316,8 @@
         for v in range(piece // 128):
             kl = kl + term[:, v * 128 : (v + 1) * 128]
         if i > 0:
-            g_chip(i - 1).start()
+            if i <= DIRECT:
+                g_chip(i - 1).start()
             g_core(i - 1).start()
     kl_p[p] = jnp.sum(kl, axis=0, keepdims=True)
     g_core(3).start()
@@ -265,9 +329,9 @@
         ]
 
     def to_plane(src_of, dst, ssem, rsem):
-        for step in range(1, plane):
-            q = (p + step) % plane
-            remote(src_of(q), dst, ssem, rsem, a, plane_peer(q)).start()
+        for step in plane_steps[:-1]:
+            q = ((yy + step[0]) % y_size) * x_size + (xx + step[2]) % x_size
+            remote(src_of(q), dst, ssem, rsem, a, moved(step)).start()
 
     for f in range(HALVES):
         cols = slice(f * n_fb * fb_width, (f + 1) * n_fb * fb_width)
@@ -304,9 +368,6 @@
     for i in range(4):
         got_core(i)
         acc[i] = outer(i, near)
-    got_chip(0)
-    got_chip(1)
-
     def r_sums(f):
         arrived(r_rsem.at[f], rs_buf.at[f])
 
@@ -328,29 +389,32 @@
         pltpu.make_async_copy(fin.at[f], block_of(gh_out, p, f), a_rsem.at[f]).start()
         drain(a_ssem.at[f], rs_buf.at[f, : plane - 1])
 
-    r_sums(0)
-    g_chip(3).start()
-    got_chip(2)
-    spread(0)
-    r_sums(1)
-
-    arrived(kp_rsem, kl_p.at[: plane - 1])
-    kl_z[zh] = jnp.sum(kl_p[...], axis=0)
-    kz_copy = remote(kl_z.at[zh], kl_z.at[zh], kz_ssem, kz_rsem, a, b_across)
-    kz_copy.start()
+    def kz_of(zz):
+        return remote(kl_z.at[zz], kl_z.at[zz], kz_ssem, kz_rsem, a, b_across)
+
+    def loss_plane(_):
+        arrived(kp_rsem, kl_p.at[: plane - 1])
+        kl_z[zh] = jnp.sum(kl_p[...], axis=0)
+        kz_of(zh).start()
+
+    def loss_across(_):
+        kz_of(1 - zh).wait_recv()
+        kl_a[a] = jnp.sum(kl_z[...], axis=0)
+        for step in range(1, 4):
+            remote(kl_a.at[a], kl_a.at[a], ka_ssem, ka_rsem, (a + step) % 4, b).start()
+
     drain(kz_ssem, kl_z.at[zh])
-    got_chip(3)
-    spread(1)
-    remote(kl_z.at[1 - zh], kl_z.at[1 - zh], kz_ssem, kz_rsem, a, b_across).wait_recv()
-    kl_a[a] = jnp.sum(kl_z[...], axis=0)
-
-    for step in range(1, 4):
-        remote(kl_a.at[a], kl_a.at[a], ka_ssem, ka_rsem, (a + step) % 4, b).start()
     drain(ka_ssem, kl_a.at[:3])
 
-    for i in range(4):
+    def far_tokens(i):
         got_pass(i)
         w_std[i, 0:share, :] = (acc[i] + outer(i, far)).astype(BF16)
+
+    for event in (ORDER + "," + ORDER_TAIL).split(","):
+        {"c": got_chip, "r": r_sums, "s": spread, "h": g_late, "m": far_tokens,
+            "p": loss_plane, "q": loss_across}[event[0]](
+            int(event[1])
+        )
     for k in range(share // sub):
         at = slice(k * sub, (k + 1) * sub)
         gw_out[at] = pltpu.einshape("idr->dir", w_std[:, at, :])

time: 51.2 us -> 45.7 us (0.89)
  Pallas kernels: 50 us -> 44.9 us
    pallas_call x1, Pallas kernels: 47.5 us -> 42.4 us  [on_device(): pl.pallas_call(functools.partial(kernel, n_ba, x_size), out_shape=(vmem((...]
where the time goes in v3:
time: 45.7 us; the launch traced here: 45.5 us
  Pallas kernels  44.9 us (98%)
  between operations  0.64 us (1%)
    pallas_call x1, Pallas kernels, on_device(): pl.pallas_call(functools.partial(kernel, n_ba, x_size), out_shape=(vmem((...  42.4 us
    pallas_call x1, Pallas kernels, on_device(): pl.pallas_call(store, out_shape=(jax.ShapeDtypeStruct((1, 1), F32), jax.S...  2.49 us

profile of v3, /device:TPU:0, one launch (start us, length us, event | category | flops | bytes accessed | tf_op | source)
XLA Modules:
  0.0 45.5 jit_solution(5478164957694826726)
XLA Ops:
  0.6 42.4 %shard_map.58 = (f32[8,128]{1,0:T(8,128)S(1)}, bf16[128,3072]{1,0:T(8,128)(2,1)S(1)}, bf16[768,4,512]{2,1,0:T(4,128)(2,1)S(1)}) custom-call(bf16[128,3072]{1,0:T(8,128)(2,1)} %hid_hbm.1, bf16[3072,1,4,512]{3,2,1,0:T(4,128)(2,1)} %w_hbm.1, bf16[16,1,32,512]{3,2,1,0:T(8,128)(2,1)} %t_hbm.1), custom_call_target="tpu_custom_call" | custom-call | tf_op jit(solution)/shard_map/pallas_call | solution.py:459
  43.0 2.5 %shard_map.59 = (f32[1,1]{1,0:T(1,128)}, bf16[128,3072]{1,0:T(8,128)(2,1)}, bf16[768,4,512]{2,1,0:T(4,128)(2,1)}) custom-call(f32[8,128]{1,0:T(8,128)S(1)} %get-tuple-element.9.div_in, bf16[128,3072]{1,0:T(8,128)(2,1)S(1)} %get-tuple-element.10.gh_in, bf16[768,4,512]{2,1,0:T(4,128)(2,1)S(1)} %get-tuple-element.11.gw_in), custom_call_target="tpu_custom_call" | custom-call | tf_op jit(solution)/shard_map/pallas_call | solution.py:508

commit v4 on v3

--- a/solution.py
+++ b/solution.py
@@ -19,7 +19,7 @@
 DIRECT = 2
 TALK_AT = 1
 ORDER = "c0,r0,h0,h1,h2,c1,r1,h3,s0,h4,h5"
-ORDER_TAIL = "r2,p0,h6,s1,h7,m0,s2,q0,m1,c2,m2,c3,m3"
+ORDER_TAIL = "r2,p0,h6,s1,h7,c2,m0,s2,q0,m1,m2,c3,m3"
 VMEM_LIMIT = 58_000_000
 TB = 16
 HALVES = 3

time: 45.7 us -> 45.7 us (level)
  no operation moved by 1% of the time
where the time goes in v4:
time: 45.7 us; the launch traced here: 45.5 us
  Pallas kernels  44.9 us (98%)
  between operations  0.64 us (1%)
    pallas_call x1, Pallas kernels, on_device(): pl.pallas_call(functools.partial(kernel, n_ba, x_size), out_shape=(vmem((...  42.4 us
    pallas_call x1, Pallas kernels, on_device(): pl.pallas_call(store, out_shape=(jax.ShapeDtypeStruct((1, 1), F32), jax.S...  2.49 us

profile of v4, /device:TPU:0, one launch (start us, length us, event | category | flops | bytes accessed | tf_op | source)
XLA Modules:
  0.0 45.5 jit_solution(14164765530843881041)
XLA Ops:
  0.6 42.4 %shard_map.58 = (f32[8,128]{1,0:T(8,128)S(1)}, bf16[128,3072]{1,0:T(8,128)(2,1)S(1)}, bf16[768,4,512]{2,1,0:T(4,128)(2,1)S(1)}) custom-call(bf16[128,3072]{1,0:T(8,128)(2,1)} %hid_hbm.1, bf16[3072,1,4,512]{3,2,1,0:T(4,128)(2,1)} %w_hbm.1, bf16[16,1,32,512]{3,2,1,0:T(8,128)(2,1)} %t_hbm.1), custom_call_target="tpu_custom_call" | custom-call | tf_op jit(solution)/shard_map/pallas_call | solution.py:459
  43.0 2.5 %shard_map.59 = (f32[1,1]{1,0:T(1,128)}, bf16[128,3072]{1,0:T(8,128)(2,1)}, bf16[768,4,512]{2,1,0:T(4,128)(2,1)}) custom-call(f32[8,128]{1,0:T(8,128)S(1)} %get-tuple-element.9.div_in, bf16[128,3072]{1,0:T(8,128)(2,1)S(1)} %get-tuple-element.10.gh_in, bf16[768,4,512]{2,1,0:T(4,128)(2,1)S(1)} %get-tuple-element.11.gw_in), custom_call_target="tpu_custom_call" | custom-call | tf_op jit(solution)/shard_map/pallas_call | solution.py:508

commit v5 on v3

--- a/solution.py
+++ b/solution.py
@@ -16,6 +16,8 @@
 HIDDEN_AT = 6
 AHEAD = 3
 LOADS_AFTER = 36
+EARLY = 2
+FIRST = 24
 DIRECT = 2
 TALK_AT = 1
 ORDER = "c0,r0,h0,h1,h2,c1,r1,h3,s0,h4,h5"
@@ -192,8 +194,8 @@
 
     t_dst = t_in.at[a, pl.ds(pl.multiple_of(t_slot * TB, TB), TB)]
 
-    def to_owner(src_of, dst, ssem, rsem):
-        for step in steps:
+    def to_owner(which, src_of, dst, ssem, rsem):
+        for step in which:
             k = moved(step)
             copy = remote(src_of(k), dst, ssem, rsem, t_owner, k)
             if step != (0, 0, 0):
@@ -211,16 +213,17 @@
     def talk():
         expected = 2 * n_ba - 1 + 5 - jnp.where(t_owner == a, 1, 0)
         pl.semaphore_wait(barrier, expected)
-        to_owner(lambda k: t_send.at[k], t_dst, t_ssem, t_rsem)
-        to_owner(lambda k: n_send, n_in.at[a, t_slot], n_ssem, n_rsem)
+        to_owner(steps, lambda k: n_send, n_in.at[a, t_slot], n_ssem, n_rsem)
+        to_owner(steps[:FIRST], lambda k: t_send.at[k], t_dst, t_ssem, t_rsem)
 
     drain_t(t_ssem, t_send)
     drain_t(n_ssem, lse_buf)
-    pl.when(zh != 0)(talk)
+    early = jnp.logical_or(zh == 0, xx < EARLY)
+    pl.when(jnp.logical_not(early))(talk)
     h_load.wait()
     for part_of in range(2):
         if part_of == TALK_AT:
-            pl.when(zh == 0)(talk)
+            pl.when(early)(talk)
         for k in range(part_of * N_CHUNKS // 2, (part_of + 1) * N_CHUNKS // 2):
             w_load(k).wait()
             if k + AHEAD < N_CHUNKS:
@@ -240,6 +243,7 @@
     for step in steps[:-1]:
         remote(lse_buf.at[b], lse_buf.at[b], s_ssem, s_rsem, a, moved(step)).start()
     drain(s_ssem, lse_buf.at[: n_ba - 1])
+    to_owner(steps[FIRST:], lambda k: t_send.at[k], t_dst, t_ssem, t_rsem)
 
     mine = pl.ds(pl.multiple_of(a * rows, rows), rows)
 
@@ -271,14 +275,14 @@
     def arrived(sem, like):
         remote(like, like, sem, sem, a, b).wait_recv()
 
+    arrived(t_rsem, t_in)
+    arrived(n_rsem, n_in)
     arrived(s_rsem, lse_buf.at[: n_ba - 1])
     parts = lse_buf[...]
     s_top = jnp.max(parts, axis=0)
     s_lse = s_top + jnp.log(jnp.sum(jnp.exp(parts - s_top[None]), axis=0))
     s_lse = lanes_to_rows(s_lse, rows)[:, 0:1]
 
-    arrived(t_rsem, t_in)
-    arrived(n_rsem, n_in)
     t_parts = jnp.sum(n_in[...], axis=1)
     t_top = jnp.max(t_parts, axis=0)
     t_all = t_top + jnp.log(jnp.sum(jnp.exp(t_parts - t_top[None]), axis=0))

time: 45.7 us -> 46.1 us (level)
  Pallas kernels: 44.9 us -> 45.4 us
    pallas_call x1, Pallas kernels: 42.4 us -> 42.9 us  [on_device(): pl.pallas_call(functools.partial(kernel, n_ba, x_size), out_shape=(vmem((...]
where the time goes in v5:
time: 46.1 us; the launch traced here: 46 us
  Pallas kernels  45.4 us (98%)
  between operations  0.64 us (1%)
    pallas_call x1, Pallas kernels, on_device(): pl.pallas_call(functools.partial(kernel, n_ba, x_size), out_shape=(vmem((...  42.9 us
    pallas_call x1, Pallas kernels, on_device(): pl.pallas_call(store, out_shape=(jax.ShapeDtypeStruct((1, 1), F32), jax.S...  2.49 us

profile of v5, /device:TPU:0, one launch (start us, length us, event | category | flops | bytes accessed | tf_op | source)
XLA Modules:
  0.0 46.0 jit_solution(4547539555703451754)
XLA Ops:
  0.6 42.9 %shard_map.58 = (f32[8,128]{1,0:T(8,128)S(1)}, bf16[128,3072]{1,0:T(8,128)(2,1)S(1)}, bf16[768,4,512]{2,1,0:T(4,128)(2,1)S(1)}) custom-call(bf16[128,3072]{1,0:T(8,128)(2,1)} %hid_hbm.1, bf16[3072,1,4,512]{3,2,1,0:T(4,128)(2,1)} %w_hbm.1, bf16[16,1,32,512]{3,2,1,0:T(8,128)(2,1)} %t_hbm.1), custom_call_target="tpu_custom_call" | custom-call | tf_op jit(solution)/shard_map/pallas_call | solution.py:463
  43.5 2.5 %shard_map.59 = (f32[1,1]{1,0:T(1,128)}, bf16[128,3072]{1,0:T(8,128)(2,1)}, bf16[768,4,512]{2,1,0:T(4,128)(2,1)}) custom-call(f32[8,128]{1,0:T(8,128)S(1)} %get-tuple-element.9.div_in, bf16[128,3072]{1,0:T(8,128)(2,1)S(1)} %get-tuple-element.10.gh_in, bf16[768,4,512]{2,1,0:T(4,128)(2,1)S(1)} %get-tuple-element.11.gw_in), custom_call_target="tpu_custom_call" | custom-call | tf_op jit(solution)/shard_map/pallas_call | solution.py:512
